TPU v7x, 256 devices: a whole 4x4x8 slice. The times are simulated.
256 devices in a mesh: wide: 32 (over x, y, core), narrow: 8 (over z).
Axes of the slice: x: 4, y: 4, z: 8, core: 2. Of those that a mesh axis runs over, the one named last changes fastest.
Arguments:
- momentum: float32 [9216, 9216], P('wide', 'narrow'), may hold values from -3 to 3
- gradient: bfloat16 [9216, 9216], P('wide', 'narrow'), may hold values from -48 to 48
- right_factor: float32 [512, 9216], P('wide', 'narrow'), may hold values from -6 to 6
Outputs:
- new_momentum: float32 [9216, 9216], P('wide', 'narrow')
- new_right: float32 [512, 9216], P('wide', 'narrow')
- update: bfloat16 [9216, 9216], P('wide', 'narrow')
All inputs are finite; a program needn't handle non-finite values.
Results may differ from a plain program's by a relative error of at most 0.001.
Values sent between devices are 32-bit elements; how exact they have to be, the bound alone decides.
A program may use at most 64 MiB of HBM per device.

v0:
```python
import jax
import jax.numpy as jnp
from jax import lax
from jax.sharding import Mesh
from jax.sharding import PartitionSpec as P

N_COLS = 9216
WIDE = ("wide_0", "wide_1", "wide_2")


EPS = 1e-06
MU = 0.95


def sent_to_all(value, axis):
    copies = jnp.broadcast_to(value, (lax.axis_size(axis), *value.shape))
    return lax.all_to_all(copies, axis, split_axis=0, concat_axis=0, tiled=True)


def in_order(parts, dim):
    parts = jnp.moveaxis(parts, 0, dim)
    dims = parts.shape
    return parts.reshape(*dims[:dim], dims[dim] * dims[dim + 1], *dims[dim + 2 :])


def whole_of(value, axes, dim):
    far, near = axes
    parts = sent_to_all(sent_to_all(value, far), near)
    return in_order(parts.swapaxes(0, 1).reshape(-1, *value.shape), dim)


def filled_up(lines, count):
    spare = -len(lines) % count
    return jnp.pad(lines, [(0, spare)] + [(0, 0)] * (lines.ndim - 1))


def sum_by_parts(value, axis):
    lines = value.reshape(-1, *value.shape[1:][-1:])
    padded = filled_up(lines, lax.axis_size(axis))
    own = lax.psum_scatter(padded, axis, scatter_dimension=0, tiled=True)
    whole = lax.all_gather(own, axis, axis=0, tiled=True)
    return whole[: len(lines)].reshape(value.shape)


def cut_along(value, dim, count):
    dims = value.shape
    parts = value.reshape(*dims[:dim], count, dims[dim] // count, *dims[dim + 1 :])
    return jnp.moveaxis(parts, dim, 0)


def summed_on_arrival(value, axis, dim):
    count = lax.axis_size(axis)
    parts = lax.all_to_all(cut_along(value, dim, count), axis, 0, 0, tiled=True)
    return jnp.sum(parts, axis=0)


def summed_rows(value, axes, dim):
    far, near = axes
    parts = cut_along(value, dim, lax.axis_size(far))
    nearer = summed_on_arrival(parts, near, dim + 1)
    arrived = lax.all_to_all(nearer, far, split_axis=0, concat_axis=0, tiled=True)
    return arrived.sum(axis=0)


def nested_sum(value, axes):
    lines = value.reshape(-1, value.shape[-1])
    own = summed_rows(filled_up(lines, lax.axis_size(axes[0]) * lax.axis_size(axes[1])), axes, 0)
    whole = whole_of(own, axes, 0)
    return whole[: len(lines)].reshape(value.shape)


def taken_together(value, axis):
    return sent_to_all(value, axis).sum(axis=0)


def sent_together(arrays, axis, dim, along):
    columns = [a.reshape(*a.shape[:along], -1) for a in arrays]
    both = jnp.concatenate(columns, axis=along)
    filled, at, finished = (lax.all_gather(both, axis, axis=dim, tiled=True), 0, [])
    for a, column in zip(arrays, columns):
        slab = filled[..., at : at + column.shape[along]]
        finished.append(slab.reshape(*slab.shape[:along], *a.shape[along:]))
        at += column.shape[along]
    return tuple(finished)


def orthonormal(projected, gram_matrix):
    factor_lower = jnp.linalg.cholesky(gram_matrix)
    return jax.scipy.linalg.solve_triangular(factor_lower, projected.T, lower=True).T


def matmul(left, right):
    return jnp.dot(left, right, preferred_element_type=jnp.float32, precision=lax.Precision.HIGHEST)


def per_device(momentum, gradient, right_factor):
    blended = momentum + gradient.astype(jnp.float32)
    partial_left = matmul(blended, whole_of(right_factor, (("wide_0", "wide_1"), "wide_2"), 0).T)
    projected = sum_by_parts(partial_left, "narrow")
    gram_matrix = nested_sum(matmul(projected.T, projected), (("wide_0", "wide_1"), "wide_2"))
    left_basis = orthonormal(projected, gram_matrix)
    columns = left_basis
    right_block = summed_on_arrival(matmul(columns.T, blended), WIDE, 0)
    squares = taken_together(jnp.sum(right_block * right_block, axis=1), "narrow")
    root_mean = jnp.sqrt(squares / N_COLS + EPS)
    new_right = right_block / root_mean[:, None]
    pieces = sent_together((right_block, root_mean), WIDE, 0, 1)
    columns = left_basis
    normed = pieces[0] / pieces[1][:, None]
    feedback = matmul(columns, pieces[0])
    direction = matmul(columns, normed)
    new_momentum = blended - (1.0 - MU) * feedback
    return (new_momentum, new_right, direction.astype(jnp.bfloat16))


def solution(mesh):
    finer = Mesh(
        mesh.devices.reshape(4, 4, 2, mesh.shape["narrow"]),
        ("wide_0", "wide_1", "wide_2", "narrow"),
    )
    return jax.shard_map(
        per_device,
        mesh=finer,
        in_specs=(P(WIDE, "narrow"), P(WIDE, "narrow"), P(WIDE, "narrow")),
        out_specs=(P(WIDE, "narrow"), P(WIDE, "narrow"), P(WIDE, "narrow")),
        check_vma=False,
    )
```

profile of v0, /device:TPU:1, one launch (start us, length us, event | category | flops | bytes accessed | tf_op | source)
XLA Modules:
  0.0 408.2 jit_solution(3183170080742980889)
XLA Ops:
  8.1 24.7 %all_to_all.41 = f32[16,16,1152]{2,1,0:T(8,128)S(1)} all-to-all(f32[16,16,1152]{2,1,0:T(8,128)S(1)} %broadcast_in_dim.18), channel_id=1, replica_groups=mesh['wide_0'=4,'wide_1'=4,'wide_2'=2,'narrow'=8] {'wide_0','wide_1'}, dimensions={0} | all-to-all | bytes 2359296 | tf_op jit(solution)/shard_map/all_to_all | solution.py:17
  33.0 7.3 %all_to_all.42 = f32[2,16,16,1152]{3,2,1,0:T(8,128)S(1)} all-to-all(f32[2,16,16,1152]{3,2,1,0:T(8,128)S(1)} %broadcast_in_dim.19), channel_id=1, replica_groups=mesh['wide_0'=4,'wide_1'=4,'wide_2'=2,'narrow'=8] {'wide_2'}, dimensions={0} | all-to-all | bytes 4718592 | tf_op jit(solution)/shard_map/all_to_all | solution.py:17
  41.8 2.6 fusion.8
  44.5 20.3 %fusion = f32[40,512]{1,0:T(8,128)S(1)} fusion(f32[288,512]{1,0:T(8,128)S(1)} %fusion.8), kind=kCustom, calls=%all-reduce-scatter | all-reduce-scatter fusion | flops 163841 | bytes 672768
  64.8 2.8 collective-permute-start
  69.1 21.6 %all-gather = f32[8,36,512]{2,1,0:T(8,128)S(1)} all-gather(f32[1,36,512]{2,1,0:T(8,128)S(1)} %dynamic-slice_bitcast_fusion), channel_id=1, replica_groups=mesh['wide_0'=4,'wide_1'=4,'wide_2'=2,'narrow'=8] {'narrow'}, dimensions={0}, use_global_device_ids=true | all-gather | bytes 663552 | tf_op jit(solution)/shard_map/all_gather | solution.py:41
  90.8 1.8 fusion.43
  92.7 13.8 %all_to_all.43 = f32[2,16,16,512]{3,2,1,0:T(8,128)S(1)} all-to-all(f32[2,16,16,512]{3,2,1,0:T(8,128)S(1)} %bitcast.79), channel_id=1, replica_groups=mesh['wide_0'=4,'wide_1'=4,'wide_2'=2,'narrow'=8] {'wide_2'}, dimensions={0} | all-to-all | bytes 2097152 | tf_op jit(solution)/shard_map/all_to_all | solution.py:53
  106.6 13.5 %all_to_all.44 = f32[16,16,512]{2,1,0:T(8,128)S(1)} all-to-all(f32[16,16,512]{2,1,0:T(8,128)S(1)} %reduce_sum.45), channel_id=1, replica_groups=mesh['wide_0'=4,'wide_1'=4,'wide_2'=2,'narrow'=8] {'wide_0','wide_1'}, dimensions={0} | all-to-all | bytes 1048576 | tf_op jit(solution)/shard_map/all_to_all | solution.py:61
  121.0 3.7 all-to-all-start.4
  124.8 9.2 %all-to-all-done.4 = f32[16,16,512]{2,1,0:T(8,128)S(1)} async-done(((f32[16,16,512]{2,1,0:T(8,128)}), f32[16,16,512]{2,1,0:T(8,128)S(1)}, u32[]{:S(2)}, u32[]{:S(2)}) %all-to-all-start.4) | async-done | bytes 524320 | tf_op jit(solution)/shard_map/all_to_all | solution.py:17
  134.1 7.4 %all_to_all.45 = f32[2,16,16,512]{3,2,1,0:T(8,128)S(1)} all-to-all(f32[2,16,16,512]{3,2,1,0:T(8,128)S(1)} %broadcast_in_dim.21), channel_id=1, replica_groups=mesh['wide_0'=4,'wide_1'=4,'wide_2'=2,'narrow'=8] {'wide_2'}, dimensions={0} | all-to-all | bytes 2097152 | tf_op jit(solution)/shard_map/all_to_all | solution.py:17
  145.3 11.7 %cholesky.104 = f32[128,128]{1,0:T(8,128)S(1)} custom-call(f32[128,128]{1,0:T(8,128)S(1)} %cholesky.266), custom_call_target="Cholesky" | custom-call | tf_op jit(solution)/shard_map/jit(cholesky)/cholesky | solution.py:88
  157.1 9.8 %custom-call.31 = f32[1,128,128]{1,2,0:T(8,128)S(1)} custom-call(f32[1,128,128]{2,1,0:T(8,128)S(1)} %get-tuple-element.30), custom_call_target="InvertDiagBlocksLowerTriangular" | custom-call | tf_op jit(solution)/shard_map/jit(cholesky)/cholesky | solution.py:88
  169.5 11.7 %cholesky.217 = f32[128,128]{1,0:T(8,128)S(1)} custom-call(f32[128,128]{1,0:T(8,128)S(1)} %cholesky.270), custom_call_target="Cholesky" | custom-call | tf_op jit(solution)/shard_map/jit(cholesky)/cholesky | solution.py:88
  181.2 9.9 %custom-call.32 = f32[1,128,128]{1,2,0:T(8,128)S(1)} custom-call(f32[1,128,128]{2,1,0:T(8,128)S(1)} %get-tuple-element.27), custom_call_target="InvertDiagBlocksLowerTriangular" | custom-call | tf_op jit(solution)/shard_map/jit(cholesky)/cholesky | solution.py:88
  192.7 11.7 %cholesky.238 = f32[128,128]{1,0:T(8,128)S(1)} custom-call(f32[128,128]{1,0:T(8,128)S(1)} %cholesky.275), custom_call_target="Cholesky" | custom-call | tf_op jit(solution)/shard_map/jit(cholesky)/cholesky | solution.py:88
  205.2 9.8 %custom-call.33 = f32[1,128,128]{1,2,0:T(8,128)S(1)} custom-call(f32[1,128,128]{2,1,0:T(8,128)S(1)} %get-tuple-element.24), custom_call_target="InvertDiagBlocksLowerTriangular" | custom-call | tf_op jit(solution)/shard_map/jit(cholesky)/cholesky | solution.py:88
  216.5 11.7 %cholesky.255 = f32[128,128]{1,0:T(8,128)S(1)} custom-call(f32[128,128]{1,0:T(8,128)S(1)} %convolution_subtract_fusion.5), custom_call_target="Cholesky" | custom-call | tf_op jit(solution)/shard_map/jit(cholesky)/cholesky | solution.py:88
  233.4 14.1 %while.1 = (s32[]{:T(128)}, f32[512,512]{1,0:T(8,128)}, s32[4,2]{0,1:T(2,128)S(1)}, f32[4,128,128]{2,1,0:T(8,128)}, s32[]{:T(128)}) while((s32[]{:T(128)}, f32[512,512]{1,0:T(8,128)}, s32[4,2]{0,1:T(2,128)S(1)}, f32[4,128,128]{2,1,0:T(8,128)}, s32[]{:T(128)}) %tuple.32), condition=%wide.while_cond, body=%wide.while_body.sunk | while | flops 2 | bytes 132205 | solution.py:89
  234.0 2.9 bitcast_dynamic-update-slice_fusion.2
  237.5 2.9 bitcast_dynamic-update-slice_fusion.2
  241.1 2.9 bitcast_dynamic-update-slice_fusion.2
  244.6 2.8 bitcast_dynamic-update-slice_fusion.2
  247.4 40.1 %custom-call.34 = f32[4,128,128]{1,2,0:T(8,128)S(1)} custom-call(f32[4,128,128]{2,1,0:T(8,128)} %get-tuple-element.10), custom_call_target="InvertDiagBlocksLowerTriangular" | custom-call | tf_op jit(solution)/shard_map/jit(_solve_triangular)/triangular_solve | solution.py:89
  292.6 4.3 %fusion.7 = f32[512,1152]{1,0:T(8,128)S(1)} fusion(f32[288,1152]{1,0:T(8,128)S(1)} %copy-done, bf16[288,1152]{1,0:T(8,128)(2,1)S(1)} %copy-done.2, f32[128,288]{0,1:T(8,128)S(1)} %fusion.27, f32[128,288]{0,1:T(8,128)S(1)} %fusion.28, f32[128,288]{0,1:T(8,128)S(1)} %fusion.30, f32[128,288]{0,1:T(8,128)S(1)} %fusion.22), kind=kOutput, calls=%fused_computation.24 | convolution fusion | flops 2039537664 | bytes 4939776 | tf_op jit(solution)/shard_map/dot_general | solution.py:93
  296.9 35.3 %all_to_all.46 = f32[32,16,1152]{2,1,0:T(8,128)} all-to-all(f32[32,16,1152]{2,1,0:T(8,128)S(1)} %bitcast.74), channel_id=1, replica_groups=mesh['wide_0'=4,'wide_1'=4,'wide_2'=2,'narrow'=8] {'wide_0','wide_1','wi..., dimensions={0} | all-to-all | bytes 4718592 | tf_op jit(solution)/shard_map/all_to_all | solution.py:53
  332.2 1.8 reduce_sum.47
  334.1 12.3 %all_to_all.47 = f32[8,1,16]{2,1,0:T(1,128)S(1)} all-to-all(f32[8,1,16]{2,1,0:T(1,128)S(1)} %broadcast_in_dim.22), channel_id=1, replica_groups=mesh['wide_0'=4,'wide_1'=4,'wide_2'=2,'narrow'=8] {'narrow'}, dimensions={0} | all-to-all | bytes 1024 | tf_op jit(solution)/shard_map/all_to_all | solution.py:17
  347.9 43.1 %all-gather.3.cloned.1.call-done = f32[512,1153]{1,0:T(8,128)} async-done(((f32[16,1153]{1,0:T(8,128)}), f32[512,1153]{1,0:T(8,128)}) %all-gather.3.cloned.1.call-update) | async-done | bytes 2361360 | tf_op jit(solution)/shard_map/all_gather | solution.py:79
  392.0 5.5 %fusion.1 = f32[288,1152]{1,0:T(8,128)} fusion(f32[512,1153]{1,0:T(8,128)} %all-gather.3.cloned.1.call-done, f32[288,1152]{1,0:T(8,128)S(1)} %copy-done, bf16[288,1152]{1,0:T(8,128)(2,1)S(1)} %copy-done.2, f32[128,288]{0,1:T(8,128)S(1)} %fusion.27, f32[128,288]{0,1:T(8,128)S(1)} %fusion.28, f32[128,288]{0,1:T(8,128)S(1)} %fusion.30, f32[128,288]{0,1:T(8,128)S(1)} %fusion.22), kind=kOutput, calls=%fused_computation.3 | convolution fusion | flops 2040201216 | bytes 6266880 | tf_op jit(solution)/shard_map/dot_general | solution.py:93
  397.5 3.6 convolution_convert_fusion
  (75 shorter events, 27.8 us)
Async XLA Ops:
  40.3 1.3 copy-start
  40.3 1.5 copy-start.1
  41.8 25.8 %copy-start.5 = (u32[256]{0:T(256)S(1)}, u32[256]{0:T(256)}, u32[]{:S(2)}) copy-start(u32[256]{0:T(256)} %constant.174) | copy-start | bytes 3076
  64.8 4.1 %collective-permute-start = (f32[28,512]{1,0:T(8,128)S(1)}, f32[28,512]{1,0:T(8,128)S(1)}, u32[]{:S(2)}, u32[]{:S(2)}) collective-permute-start(f32[28,512]{1,0:T(8,128)S(1)} %slice.135), channel_id=1, source_target_pairs={{0,1},{1,2},{2,3},{3,4},{4,5},{5,6},{6,7},{8,9},{9,10},{10,11},{11... | collective-permute-start | bytes 172040
  121.0 13.0 %all-to-all-start.4 = ((f32[16,16,512]{2,1,0:T(8,128)}), f32[16,16,512]{2,1,0:T(8,128)S(1)}, u32[]{:S(2)}, u32[]{:S(2)}) async-start(f32[16,16,512]{2,1,0:T(8,128)} %broadcast_in_dim.20), calls=%async_computation.4 | async-start | bytes 1048576 | tf_op jit(solution)/shard_map/all_to_all | solution.py:17
  124.7 266.2 %all-gather.3.cloned.1.call-start = ((), (), s32[]{:S(2)}) async-start(), calls=%async_computation.8 | async-start | bytes 2703360 | tf_op jit(solution)/shard_map/all_gather | solution.py:79
  144.3 1.0 copy-start.3
  289.0 3.6 copy-start.2
  392.0 5.5 %copy-start.4 = (f32[512,1153]{1,0:T(8,128)S(1)}, f32[512,1153]{1,0:T(8,128)}, u32[]{:S(2)}) copy-start(f32[512,1153]{1,0:T(8,128)} %all-gather.3.cloned.1.call-done) | copy-start | bytes 7084036
Sparse Core Ops, SparseCore 0:
  347.3 43.6 all-gather.2
where the time goes:
time: 415 us; the launch traced here: 408 us
  blocking collectives  156 us (38%)
  other arithmetic  125 us (30%)
  waiting for transfers between devices  52.3 us (13%)
  matrix products  28.2 us (7%)
  local copies, waits for them, and re-layouts  22.2 us (5%)
  between operations  17.9 us (4%)
  starting transfers between devices  6.56 us (2%)
    another operation x14, other arithmetic, orthonormal(): factor_lower = jnp.linalg.cholesky(gram_matrix)  78.5 us
    all_to_all x4, blocking collectives, sent_to_all(): return lax.all_to_all(copies, axis, split_axis=0, concat_axis=0, tiled=True)  51.7 us
    all_to_all x2, blocking collectives, summed_on_arrival(): parts = lax.all_to_all(cut_along(value, dim, count), axis, 0, 0, tiled=True)  49.1 us
    all_gather x1, waiting for transfers between devices, sent_together(): lax.all_gather(both, axis, axis=dim, tiled=True)  43.1 us
    another operation x3, other arithmetic, orthonormal(): jax.scipy.linalg.solve_triangular(factor_lower, projected.T, lower=True)  41.4 us
    all_gather x1, blocking collectives, sum_by_parts(): whole = lax.all_gather(own, axis, axis=0, tiled=True)  21.6 us
    unnamed x1, blocking collectives  20.3 us
    dot_general x5, matrix products, matmul(): jnp.dot(left, right, preferred_element_type=jnp.float32, precision=lax.Pr...  17.8 us
  transfers between devices with their start and end apart: 3, of which 3 were waited for; matrix products, arithmetic and copies ran while one was open for 0% of the time, Pallas kernels for 0%

commit v1 on v0

--- a/solution.py
+++ b/solution.py
@@ -1,6 +1,8 @@
 import jax
 import jax.numpy as jnp
 from jax import lax
+from jax.experimental import pallas as pl
+from jax.experimental.pallas import tpu as pltpu
 from jax.sharding import Mesh
 from jax.sharding import PartitionSpec as P
 
@@ -84,9 +86,113 @@
     return tuple(finished)
 
 
+HI = lax.Precision.HIGHEST
+
+def lane_of(tile, lane):
+    return jnp.broadcast_to(tile[:, lane:lane + 1], tile.shape)
+
+def row_of(tile, row):
+    return jnp.broadcast_to(tile[row:row + 1, :], tile.shape)
+
+def inv_chol_block(d):
+    n = 128
+    tiles = [d[8 * i:8 * i + 8, :] for i in range(n // 8)]
+    lanes = lax.broadcasted_iota(jnp.int32, (8, n), 1)
+    subs = lax.broadcasted_iota(jnp.int32, (8, n), 0)
+    for j in range(n // 8):
+        t = tiles[j]
+        inside = (lanes >= 8 * j) & (lanes < 8 * j + 8)
+        cols = [lane_of(t, 8 * j + k) for k in range(8)]
+        e = {(i, k): row_of(cols[k], i) for k in range(8) for i in range(k, 8)}
+        raw = {i: [lane_of(tiles[i], 8 * j + k) for k in range(8)] for i in range(j + 1, n // 8)}
+        own = jnp.where(inside, jnp.where(lanes - 8 * j == subs, 1.0, 0.0), t)
+        rows = [row_of(own, k) for k in range(8)]
+        scale, low = [], {}
+        for k in range(8):
+            scale.append(lax.rsqrt(e[k, k]))
+            for i in range(k + 1, 8):
+                low[i, k] = e[i, k] * scale[k]
+            for i in range(k + 1, 8):
+                for m in range(k + 1, i + 1):
+                    e[i, m] = e[i, m] - low[i, k] * low[m, k]
+        def forward(values):
+            out = []
+            for k in range(8):
+                v = values[k]
+                for m in range(k):
+                    v = v - low[k, m] * out[m]
+                out.append(v * scale[k])
+            return out
+        up = forward(rows)
+        new = up[0]
+        for k in range(1, 8):
+            new = jnp.where(subs == k, up[k], new)
+        tiles[j] = new
+        for i in range(j + 1, n // 8):
+            c = forward(raw[i])
+            v = jnp.where(inside, 0.0, tiles[i])
+            for k in range(8):
+                v = v - c[k] * up[k]
+            tiles[i] = v
+    x = jnp.concatenate(tiles, axis=0)
+    r = lax.broadcasted_iota(jnp.int32, (n, n), 0)
+    c = lax.broadcasted_iota(jnp.int32, (n, n), 1)
+    return jnp.where(c <= r, x, 0.0)
+
+def dot_nt(a, b):
+    return lax.dot_general(a, b, (((1,), (1,)), ((), ())), precision=HI, preferred_element_type=jnp.float32)
+
+def dot_nn(a, b):
+    return lax.dot_general(a, b, (((1,), (0,)), ((), ())), precision=HI, preferred_element_type=jnp.float32)
+
+def inv_chol(m_ref, nb=4):
+    b = 128
+    for k in range(nb):
+        s = slice(b * k, b * k + b)
+        x = inv_chol_block(m_ref[s, s])
+        if k:
+            left = m_ref[s, :b * k]
+            left = dot_nn(x, left)
+            m_ref[s, :b * k] = left
+        m_ref[s, s] = x
+        for i in range(k + 1, nb):
+            t = slice(b * i, b * i + b)
+            c = dot_nt(m_ref[t, s], x)
+            m_ref[t, s] = c
+        for i in range(k + 1, nb):
+            t = slice(b * i, b * i + b)
+            c = m_ref[t, s]
+            for q in range(k + 1, i + 1):
+                u = slice(b * q, b * q + b)
+                m_ref[t, u] = m_ref[t, u] - dot_nt(c, m_ref[u, s])
+        for i in range(nb - 1, k, -1):
+            t = slice(b * i, b * i + b)
+            c = m_ref[t, s]
+            if k:
+                m_ref[t, :b * k] = m_ref[t, :b * k] - dot_nn(c, m_ref[s, :b * k])
+            m_ref[t, s] = -dot_nn(c, x)
+        if k:
+            pass
+    for k in range(nb):
+        for q in range(k + 1, nb):
+            m_ref[b * k:b * k + b, b * q:b * q + b] = jnp.zeros((b, b), jnp.float32)
+
+def kernel(g_ref, x_ref):
+    x_ref[...] = g_ref[...]
+    inv_chol(x_ref)
+
+def inverse_factor(g):
+    return pl.pallas_call(
+        kernel,
+        out_shape=jax.ShapeDtypeStruct((512, 512), jnp.float32),
+        in_specs=[pl.BlockSpec(memory_space=pltpu.VMEM)],
+        out_specs=pl.BlockSpec(memory_space=pltpu.VMEM),
+        compiler_params=pltpu.CompilerParams(vmem_limit_bytes=32 << 20),
+    )(g)
+
+
 def orthonormal(projected, gram_matrix):
-    factor_lower = jnp.linalg.cholesky(gram_matrix)
-    return jax.scipy.linalg.solve_triangular(factor_lower, projected.T, lower=True).T
+    return dot_nt(projected, inverse_factor(gram_matrix))
 
 
 def matmul(left, right):

time: 415 us -> 285 us (0.69); the launches traced: 408 us -> 284 us
  other arithmetic: 125 us -> 5.49 us
  Pallas kernels: 0 us -> 20.4 us
  local copies, waits for them, and re-layouts: 22.2 us -> 6.05 us
  blocking collectives: 156 us -> 172 us
  matrix products: 28.2 us -> 19 us
  waiting for transfers between devices: 52.3 us -> 43.1 us
    another operation x17 -> x0, other arithmetic: 120 us -> none  [the longest x14 78.5 us: orthonormal(): factor_lower = jnp.linalg.cholesky(gram_matrix)]
    pallas_call x0 -> x1, Pallas kernels: none -> 20.4 us  [inverse_factor(): pl.pallas_call(kernel, out_shape=jax.ShapeDtypeStruct((512, 512), jnp.flo...]
    another operation x18 -> x0, local copies, waits for them, and re-layouts: 15.5 us -> none
    all_to_all x4 -> x5, blocking collectives: 51.7 us -> 64.3 us  [sent_to_all(): return lax.all_to_all(copies, axis, split_axis=0, concat_axis=0, tiled=True)]
    another operation x13 -> x0, matrix products: 10.5 us -> none  [the longest x6 5.47 us: orthonormal(): factor_lower = jnp.linalg.cholesky(gram_matrix)]
    all_to_all x1 -> x0, waiting for transfers between devices: 9.16 us -> none  [sent_to_all(): return lax.all_to_all(copies, axis, split_axis=0, concat_axis=0, tiled=True)]
  transfers between devices with their start and end apart: 3 -> 2, of which waited for: 3 -> 2; matrix products, arithmetic and copies ran while one was open for 0% -> 0% of each run, Pallas kernels for 0% -> 0%
where the time goes in v1:
time: 285 us; the launch traced here: 284 us
  blocking collectives  172 us (60%)
  waiting for transfers between devices  43.1 us (15%)
  Pallas kernels  20.4 us (7%)
  matrix products  19 us (7%)
  between operations  14.8 us (5%)
  local copies, waits for them, and re-layouts  6.05 us (2%)
  other arithmetic  5.49 us (2%)
    all_to_all x5, blocking collectives, sent_to_all(): return lax.all_to_all(copies, axis, split_axis=0, concat_axis=0, tiled=True)  64.3 us
    all_to_all x2, blocking collectives, summed_on_arrival(): parts = lax.all_to_all(cut_along(value, dim, count), axis, 0, 0, tiled=True)  50.5 us
    all_gather x1, waiting for transfers between devices, sent_together(): lax.all_gather(both, axis, axis=dim, tiled=True)  43.1 us
    all_gather x1, blocking collectives, sum_by_parts(): whole = lax.all_gather(own, axis, axis=0, tiled=True)  23 us
    pallas_call x1, Pallas kernels, inverse_factor(): pl.pallas_call(kernel, out_shape=jax.ShapeDtypeStruct((512, 512), jnp.flo...  20.4 us
    unnamed x1, blocking collectives  20.3 us
    dot_general x5, matrix products, matmul(): jnp.dot(left, right, preferred_element_type=jnp.float32, precision=lax.Pr...  17.8 us
    all_to_all x1, blocking collectives, summed_rows(): lax.all_to_all(nearer, far, split_axis=0, concat_axis=0, tiled=True)  14 us
  transfers between devices with their start and end apart: 2, of which 2 were waited for; matrix products, arithmetic and copies ran while one was open for 0% of the time, Pallas kernels for 0%

profile of v1, /device:TPU:1, one launch (start us, length us, event | category | flops | bytes accessed | tf_op | source)
XLA Modules:
  0.0 283.8 jit_solution(5411325527910486168)
XLA Ops:
  7.2 1.0 broadcast_in_dim.16
  8.2 24.7 %all_to_all.41 = f32[16,16,1152]{2,1,0:T(8,128)S(1)} all-to-all(f32[16,16,1152]{2,1,0:T(8,128)S(1)} %broadcast_in_dim.16), channel_id=1, replica_groups=mesh['wide_0'=4,'wide_1'=4,'wide_2'=2,'narrow'=8] {'wide_0','wide_1'}, dimensions={0} | all-to-all | bytes 2359296 | tf_op jit(solution)/shard_map/all_to_all | solution.py:19
  32.9 0.2 broadcast_in_dim.17
  33.1 7.3 %all_to_all.42 = f32[2,16,16,1152]{3,2,1,0:T(8,128)S(1)} all-to-all(f32[2,16,16,1152]{3,2,1,0:T(8,128)S(1)} %broadcast_in_dim.17), channel_id=1, replica_groups=mesh['wide_0'=4,'wide_1'=4,'wide_2'=2,'narrow'=8] {'wide_2'}, dimensions={0} | all-to-all | bytes 4718592 | tf_op jit(solution)/shard_map/all_to_all | solution.py:19
  40.4 0.2 copy.16
  40.6 1.1 copy-done
  41.7 0.2 copy-done.1
  41.9 2.6 fusion.7
  44.5 20.3 %fusion = f32[40,512]{1,0:T(8,128)S(1)} fusion(f32[288,512]{1,0:T(8,128)S(1)} %fusion.7), kind=kCustom, calls=%all-reduce-scatter | all-reduce-scatter fusion | flops 163841 | bytes 672768
  64.8 2.8 collective-permute-start
  67.6 0.6 dynamic-slice.4
  68.9 0.1 concatenate.4
  69.1 23.0 %all-gather = f32[8,36,512]{2,1,0:T(8,128)} all-gather(f32[1,36,512]{2,1,0:T(8,128)S(1)} %dynamic-slice_bitcast_fusion), channel_id=1, replica_groups=mesh['wide_0'=4,'wide_1'=4,'wide_2'=2,'narrow'=8] {'narrow'}, dimensions={0}, use_global_device_ids=true | all-gather | bytes 663552 | tf_op jit(solution)/shard_map/all_gather | solution.py:43
  92.1 1.1 reshape.34
  93.3 1.9 fusion.9
  95.3 15.2 %all_to_all.43 = f32[2,16,16,512]{3,2,1,0:T(8,128)} all-to-all(f32[2,16,16,512]{3,2,1,0:T(8,128)S(1)} %bitcast.29), channel_id=1, replica_groups=mesh['wide_0'=4,'wide_1'=4,'wide_2'=2,'narrow'=8] {'wide_2'}, dimensions={0} | all-to-all | bytes 2097152 | tf_op jit(solution)/shard_map/all_to_all | solution.py:55
  110.5 2.1 reduce_sum.45
  112.6 14.0 %all_to_all.44 = f32[16,16,512]{2,1,0:T(8,128)S(1)} all-to-all(f32[16,16,512]{2,1,0:T(8,128)} %reduce_sum.45), channel_id=1, replica_groups=mesh['wide_0'=4,'wide_1'=4,'wide_2'=2,'narrow'=8] {'wide_0','wide_1'}, dimensions={0} | all-to-all | bytes 1048576 | tf_op jit(solution)/shard_map/all_to_all | solution.py:63
  126.7 12.5 %all_to_all.45 = f32[16,16,512]{2,1,0:T(8,128)S(1)} all-to-all(f32[16,16,512]{2,1,0:T(8,128)S(1)} %broadcast_in_dim.18), channel_id=1, replica_groups=mesh['wide_0'=4,'wide_1'=4,'wide_2'=2,'narrow'=8] {'wide_0','wide_1'}, dimensions={0} | all-to-all | bytes 1048576 | tf_op jit(solution)/shard_map/all_to_all | solution.py:19
  139.4 7.7 %all_to_all.46 = f32[2,16,16,512]{3,2,1,0:T(8,128)S(1)} all-to-all(f32[2,16,16,512]{3,2,1,0:T(8,128)S(1)} %broadcast_in_dim.19), channel_id=1, replica_groups=mesh['wide_0'=4,'wide_1'=4,'wide_2'=2,'narrow'=8] {'wide_2'}, dimensions={0} | all-to-all | bytes 2097152 | tf_op jit(solution)/shard_map/all_to_all | solution.py:19
  147.2 20.4 %shard_map.58 = f32[512,512]{1,0:T(8,128)S(1)} custom-call(f32[512,512]{1,0:T(8,128)S(1)} %bitcast.26), custom_call_target="tpu_custom_call" | custom-call | tf_op jit(solution)/shard_map/pallas_call | solution.py:185
  167.6 1.2 fusion.10
  168.8 4.3 %fusion.6 = f32[512,1152]{1,0:T(8,128)S(1)} fusion(f32[288,512]{1,0:T(8,128)S(1)} %fusion.10, f32[288,1152]{1,0:T(8,128)S(1)} %copy-done, bf16[288,1152]{1,0:T(8,128)(2,1)S(1)} %copy-done.1), kind=kOutput, calls=%fused_computation.9 | convolution fusion | flops 2039095296 | bytes 4939776 | tf_op jit(solution)/shard_map/dot_general | solution.py:199
  173.1 35.3 %all_to_all.47 = f32[32,16,1152]{2,1,0:T(8,128)} all-to-all(f32[32,16,1152]{2,1,0:T(8,128)S(1)} %bitcast.28), channel_id=1, replica_groups=mesh['wide_0'=4,'wide_1'=4,'wide_2'=2,'narrow'=8] {'wide_0','wide_1','wi..., dimensions={0} | all-to-all | bytes 4718592 | tf_op jit(solution)/shard_map/all_to_all | solution.py:55
  208.4 1.8 reduce_sum.47
  210.3 12.0 %all_to_all.48 = f32[8,1,16]{2,1,0:T(1,128)S(1)} all-to-all(f32[8,1,16]{2,1,0:T(1,128)S(1)} %broadcast_in_dim.20), channel_id=1, replica_groups=mesh['wide_0'=4,'wide_1'=4,'wide_2'=2,'narrow'=8] {'narrow'}, dimensions={0} | all-to-all | bytes 1024 | tf_op jit(solution)/shard_map/all_to_all | solution.py:19
  222.4 0.6 pad_maximum_fusion
  223.0 0.7 broadcast_divide_fusion
  223.7 43.1 %all-gather.3.cloned.1.call-done = f32[512,1153]{1,0:T(8,128)} async-done(((f32[16,1153]{1,0:T(8,128)}), f32[512,1153]{1,0:T(8,128)}) %all-gather.3.cloned.1.call-update) | async-done | bytes 2361360 | tf_op jit(solution)/shard_map/all_gather | solution.py:81
  266.8 1.1 slice_reduce_fusion
  267.9 5.5 %fusion.1 = f32[288,1152]{1,0:T(8,128)} fusion(f32[288,512]{1,0:T(8,128)S(1)} %fusion.10, f32[512,1153]{1,0:T(8,128)} %all-gather.3.cloned.1.call-done, f32[288,1152]{1,0:T(8,128)S(1)} %copy-done, bf16[288,1152]{1,0:T(8,128)(2,1)S(1)} %copy-done.1), kind=kOutput, calls=%fused_computation.1 | convolution fusion | flops 2039758848 | bytes 6266880 | tf_op jit(solution)/shard_map/dot_general | solution.py:199
  273.4 3.5 %convolution_convert_fusion = bf16[288,1152]{1,0:T(8,128)(2,1)} fusion(f32[288,512]{1,0:T(8,128)S(1)} %fusion.10, f32[512,1153]{1,0:T(8,128)S(1)} %copy-done.2, f32[512]{0:T(512)S(1)} %slice_reduce_fusion), kind=kOutput, calls=%fused_computation.2 | convolution fusion | flops 2039353344 | bytes 3614720 | tf_op jit(solution)/shard_map/dot_general | solution.py:199
  (21 shorter events, 0.8 us)
Async XLA Ops:
  7.2 259.6 %all-gather.3.cloned.1.call-start = ((), (), s32[]{:S(2)}) async-start(), calls=%async_computation.8 | async-start | bytes 2703360 | tf_op jit(solution)/shard_map/all_gather | solution.py:81
  40.4 1.3 copy-start
  40.4 1.5 copy-start.1
  41.9 25.8 %copy-start.3 = (u32[256]{0:T(256)S(1)}, u32[256]{0:T(256)}, u32[]{:S(2)}) copy-start(u32[256]{0:T(256)} %constant.13) | copy-start | bytes 3076
  64.8 4.1 %collective-permute-start = (f32[28,512]{1,0:T(8,128)S(1)}, f32[28,512]{1,0:T(8,128)S(1)}, u32[]{:S(2)}, u32[]{:S(2)}) collective-permute-start(f32[28,512]{1,0:T(8,128)S(1)} %slice.10), channel_id=1, source_target_pairs={{0,1},{1,2},{2,3},{3,4},{4,5},{5,6},{6,7},{8,9},{9,10},{10,11},{11... | collective-permute-start | bytes 172040
  267.9 5.5 %copy-start.2 = (f32[512,1153]{1,0:T(8,128)S(1)}, f32[512,1153]{1,0:T(8,128)}, u32[]{:S(2)}) copy-start(f32[512,1153]{1,0:T(8,128)} %all-gather.3.cloned.1.call-done) | copy-start | bytes 7084036
Sparse Core Ops, SparseCore 0:
  223.2 43.6 all-gather.2
